TPU v7x, 32 devices: a whole 2x2x4 slice. The times are simulated.
32 devices in a mesh: orb: 4 (over z), tile: 8 (over y, x, core).
Axes of the slice: x: 2, y: 2, z: 4, core: 2. Of those that a mesh axis runs over, the one named last changes fastest.
Arguments:
- basis_values: bfloat16 [2048, 65536], P('tile'), may hold values from -6 to 6
- coefficients: bfloat16 [65536, 128], P('tile', 'orb'), may hold values from -0.03125 to 0.03125
- occupations: float32 [128], P('orb'), may hold values from 0.5 to 2
- owners: int32 [2048, 1], P('tile'), may hold values from 0 to 7; in each aligned block of 256 rows (0 to 255, 256 to 511, ...) at most 64 rows name the same one
- offsets: int32 [2048], P('tile'), may hold values from 0 to 8191
Outputs:
- density: float32 [64, 64, 128], P('tile', 'orb')
- gradient: float32 [3, 64, 64, 128], P(None, 'tile', 'orb')
Inputs may be any that keep to these rules, and one draw needn't show every extreme that they name: `owners`: at most 64 entries of one tile's list name the same owner, and some tile's list reaches 64.
All inputs are finite; a program needn't handle non-finite values.
Results may differ from a plain program's by a relative error of at most 0.0003.
Values may be sent and summed in bfloat16 or wider, within the bound.
A program may use at most 320 MiB of HBM per device.

v0:
```python
import jax
import jax.numpy as jnp
from jax import lax
from jax.sharding import PartitionSpec as P

CY = 64
CZ = 128


def with_halo(cells, sides, width):
    for axis, dim in sides:
        count = lax.axis_size(axis)
        ends = count - 1
        head = lax.slice_in_dim(cells, 0, width, axis=dim)
        tail = lax.slice_in_dim(cells, cells.shape[dim] - width, cells.shape[dim], axis=dim)
        cells = jnp.concatenate(
            [
                lax.ppermute(tail, axis, [(i, (i + 1) % count) for i in range(ends)]),
                cells,
                lax.ppermute(head, axis, [((i + 1) % count, i) for i in range(ends)]),
            ],
            axis=dim,
        )
    return cells


def central(padded):
    along_x = 0.5 * (padded[2:, 1:-1, 1:-1] - padded[:-2, 1:-1, 1:-1])
    along_y = 0.5 * (padded[1:-1, 2:, 1:-1] - padded[1:-1, :-2, 1:-1])
    along_z = 0.5 * (padded[1:-1, 1:-1, 2:] - padded[1:-1, 1:-1, :-2])
    return jnp.stack([along_x, along_y, along_z])


def body(basis_values, coefficients, occupations, owners, offsets):
    listed_count = owners.shape[0]
    rows_held = coefficients.shape[0]
    local_orbitals = coefficients.shape[1]
    owner_ids = owners[:, 0]
    global_rows = owner_ids * rows_held + offsets
    empty = jnp.zeros((listed_count, local_orbitals), jnp.bfloat16)
    shard_rows = lax.all_gather(coefficients, "tile", axis=0, tiled=True)
    inside = (global_rows >= 0) & (global_rows < shard_rows.shape[0])
    safe_rows = jnp.clip(global_rows, 0, shard_rows.shape[0] - 1)
    taken = jnp.take(shard_rows, safe_rows, axis=0)
    listed = jnp.where(inside[:, None], taken, empty)
    depth_cells = basis_values.shape[1] // (CY * CZ)
    share_width = CY // lax.axis_size("orb")
    orbitals = jnp.einsum("bo,bc->oc", listed, basis_values, preferred_element_type=jnp.float32)
    partial_value = jnp.sum(occupations[:, None] * orbitals * orbitals, axis=0).reshape(
        depth_cells, CY, CZ
    )
    density_full = lax.psum(partial_value, "orb")
    padded = with_halo(density_full, (("tile", 0),), 1)
    padded = jnp.pad(padded, ((0, 0), (1, 1), (1, 1)))
    first_col = lax.axis_index("orb") * share_width
    density = lax.dynamic_slice_in_dim(density_full, first_col, share_width, 1)
    gradient = lax.dynamic_slice_in_dim(central(padded), first_col, share_width, 2)
    return (density, gradient)


def solution(mesh):
    placed = (P("tile", None), P("tile", "orb"), P("orb"), P("tile", None), P("tile"))
    return jax.shard_map(
        body,
        mesh=mesh,
        in_specs=placed,
        out_specs=(P("tile", "orb", None), P(None, "tile", "orb", None)),
        check_vma=False,
    )
```

profile of v0, /device:TPU:4, one launch (start us, length us, event | category | flops | bytes accessed | tf_op | source)
XLA Modules:
  0.0 181.8 jit_solution(3366293693858491619)
XLA Ops:
  7.2 0.0 all-gather.2.cloned.1.call-start
  7.2 2.7 %copy.7 = bf16[8192,32]{1,0:T(8,128)(2,1)} copy(bf16[8192,32]{0,1:T(8,128)(2,1)} %param.6) | data formatting | bytes 1048576 | tf_op args[1]
  9.9 0.0 all-gather.2.cloned.1.call-update
  9.9 0.0 all-reduce.3.cloned.1.call-start
  10.0 0.7 broadcast_multiply_fusion
  10.6 0.7 compare_and_fusion
  11.3 88.9 %all-gather.2.cloned.1.call-done = bf16[65536,32]{1,0:T(8,128)(2,1)} async-done(((bf16[8192,32]{1,0:T(8,128)(2,1)}), bf16[65536,32]{1,0:T(8,128)(2,1)}) %all-gather.2.cloned.1.call-update) | async-done | bytes 4194320 | tf_op jit(solution)/shard_map/all_gather | solution.py:41
  100.3 8.7 %gather_fusion = bf16[256,32]{1,0:T(8,128)(2,1)S(1)} fusion(bf16[65536,32]{1,0:T(8,128)(2,1)} %all-gather.2.cloned.1.call-done, s32[1024]{0:T(1024)S(1)} %pad_clamp_fusion), kind=kCustom, calls=%fused_computation | custom fusion | bytes 33792 | tf_op jit(solution)/shard_map/jit(_take)/gather | solution.py:44
  108.9 17.4 %fusion = f32[65536]{0:T(1024)} fusion(f32[32]{0:T(128)} %param.7, bf16[256,65536]{1,0:T(8,128)(2,1)} %param.5, bf16[256,32]{1,0:T(8,128)(2,1)S(1)} %gather_fusion, pred[256]{0:T(512)(128)(4,1)S(1)} %get-tuple-element.2, pred[256]{0:T(512)(128)(4,1)S(1)} %get-tuple-element.8), kind=kOutput, calls=%fused_computation.2 | convolution fusion | flops 1079984128 | bytes 33833600 | tf_op jit(solution)/shard_map/bo,bc->oc/dot_general | solution.py:48
  126.3 0.0 all-reduce.3.cloned.1.call-update
  126.4 36.5 %all-reduce.3.cloned.1.call-done = f32[8,64,128]{2,1,0:T(8,128)} async-done(((f32[8,64,128]{2,1,0:T(8,128)}), f32[8,64,128]{2,1,0:T(8,128)}) %all-reduce.3.cloned.1.call-update) | async-done | bytes 262160 | tf_op jit(solution)/shard_map/psum | solution.py:52
  162.8 0.8 fusion.24
  163.6 1.9 %collective-permute-start = (f32[1,64,128]{2,1,0:T(8,128)S(1)}, f32[1,64,128]{2,1,0:T(8,128)S(1)}, u32[]{:S(2)}, u32[]{:S(2)}) collective-permute-start(f32[1,64,128]{2,1,0:T(8,128)S(1)} %get-tuple-element.6), channel_id=1, source_target_pairs={{1,0},{2,1},{3,2},{4,3},{5,4},{6,5},{7,6},{9,8},{10,9},{11,10},{12... | collective-permute-start | bytes 98312 | tf_op jit(solution)/shard_map/ppermute | solution.py:20
  165.5 2.4 %collective-permute-start.1 = (f32[1,64,128]{2,1,0:T(8,128)S(1)}, f32[1,64,128]{2,1,0:T(8,128)S(1)}, u32[]{:S(2)}, u32[]{:S(2)}) collective-permute-start(f32[1,64,128]{2,1,0:T(8,128)S(1)} %get-tuple-element.7), channel_id=1, source_target_pairs={{0,1},{1,2},{2,3},{3,4},{4,5},{5,6},{6,7},{8,9},{9,10},{10,11},{11... | collective-permute-start | bytes 98312 | tf_op jit(solution)/shard_map/ppermute | solution.py:18
  167.9 1.5 constant_dynamic-slice_fusion
  169.4 0.0 collective-permute-done
  169.4 2.2 %collective-permute-done.1 = f32[1,64,128]{2,1,0:T(8,128)S(1)} collective-permute-done((f32[1,64,128]{2,1,0:T(8,128)S(1)}, f32[1,64,128]{2,1,0:T(8,128)S(1)}, u32[]{:S(2)}, u32[]{:S(2)}) %collective-permute-start.1) | collective-permute-done | bytes 32800 | tf_op jit(solution)/shard_map/ppermute | solution.py:18
  171.7 1.2 select_maximum_fusion
  172.9 1.3 fusion.5
  174.2 0.7 fusion.12
  (1 shorter events, 0.0 us)
Async XLA Ops:
  7.2 93.1 %all-gather.2.cloned.1.call-start = ((), (), s32[]{:S(2)}) async-start(), calls=%async_computation | async-start | bytes 18874368 | tf_op jit(solution)/shard_map/all_gather | solution.py:41
  9.9 152.9 %all-reduce.3.cloned.1.call-start = ((), (), s32[]{:S(2)}) async-start(), calls=%async_computation.1 | async-start | bytes 524288 | tf_op jit(solution)/shard_map/psum | solution.py:52
  163.6 5.8 %collective-permute-start = (f32[1,64,128]{2,1,0:T(8,128)S(1)}, f32[1,64,128]{2,1,0:T(8,128)S(1)}, u32[]{:S(2)}, u32[]{:S(2)}) collective-permute-start(f32[1,64,128]{2,1,0:T(8,128)S(1)} %get-tuple-element.6), channel_id=1, source_target_pairs={{1,0},{2,1},{3,2},{4,3},{5,4},{6,5},{7,6},{9,8},{10,9},{11,10},{12... | collective-permute-start | bytes 98312 | tf_op jit(solution)/shard_map/ppermute | solution.py:20
  165.5 6.1 %collective-permute-start.1 = (f32[1,64,128]{2,1,0:T(8,128)S(1)}, f32[1,64,128]{2,1,0:T(8,128)S(1)}, u32[]{:S(2)}, u32[]{:S(2)}) collective-permute-start(f32[1,64,128]{2,1,0:T(8,128)S(1)} %get-tuple-element.7), channel_id=1, source_target_pairs={{0,1},{1,2},{2,3},{3,4},{4,5},{5,6},{6,7},{8,9},{9,10},{10,11},{11... | collective-permute-start | bytes 98312 | tf_op jit(solution)/shard_map/ppermute | solution.py:18
Sparse Core Ops, SparseCore 0:
  10.0 90.1 all-gather.1
  126.5 36.3 all-reduce.2
where the time goes:
time: 182 us
  waiting for transfers between devices  128 us (70%)
  matrix products  17.4 us (10%)
  between operations  14.1 us (8%)
  local copies, waits for them, and re-layouts  13.6 us (7%)
  other arithmetic  4.62 us (3%)
  starting transfers between devices  4.39 us (2%)
    all_gather x1, waiting for transfers between devices, body(): shard_rows = lax.all_gather(coefficients, 'tile', axis=0, tiled=True)  88.9 us
    psum x1, waiting for transfers between devices, body(): density_full = lax.psum(partial_value, 'orb')  36.5 us
    dot_general x1, matrix products, body(): jnp.einsum('bo,bc->oc', listed, basis_values, preferred_element_type=jnp....  17.4 us
    gather x1, local copies, waits for them, and re-layouts, body(): taken = jnp.take(shard_rows, safe_rows, axis=0)  8.65 us
  transfers between devices with their start and end apart: 4, of which 3 were waited for; matrix products, arithmetic and copies ran while one was open for 2% of the time, Pallas kernels for 0%

commit v1 on v0

--- a/solution.py
+++ b/solution.py
@@ -5,6 +5,12 @@
 
 CY = 64
 CZ = 128
+
+
+def tell_stages_all_on(local_x):
+    later = jax.lax.all_gather(local_x, "orb")
+    w2 = jnp.sum(later, axis=0)
+    return w2
 
 
 def with_halo(cells, sides, width):
@@ -49,7 +55,7 @@
     partial_value = jnp.sum(occupations[:, None] * orbitals * orbitals, axis=0).reshape(
         depth_cells, CY, CZ
     )
-    density_full = lax.psum(partial_value, "orb")
+    density_full = tell_stages_all_on(partial_value)
     padded = with_halo(density_full, (("tile", 0),), 1)
     padded = jnp.pad(padded, ((0, 0), (1, 1), (1, 1)))
     first_col = lax.axis_index("orb") * share_width

time: 182 us -> 173 us (0.951)
  waiting for transfers between devices: 128 us -> 121 us
    psum x1 -> x0, waiting for transfers between devices: 36.5 us -> none  [body(): density_full = lax.psum(partial_value, 'orb')]
    all_gather x0 -> x1, waiting for transfers between devices: none -> 28.9 us  [tell_stages_all_on(): later = jax.lax.all_gather(local_x, 'orb')]
  transfers between devices with their start and end apart: 4 -> 4, of which waited for: 3 -> 3; matrix products, arithmetic and copies ran while one was open for 2% -> 1% of each run, Pallas kernels for 0% -> 0%
where the time goes in v1:
time: 173 us
  waiting for transfers between devices  121 us (70%)
  matrix products  17.4 us (10%)
  between operations  14.1 us (8%)
  local copies, waits for them, and re-layouts  12 us (7%)
  starting transfers between devices  4.41 us (3%)
  other arithmetic  3.92 us (2%)
    all_gather x1, waiting for transfers between devices, body(): shard_rows = lax.all_gather(coefficients, 'tile', axis=0, tiled=True)  88.9 us
    all_gather x1, waiting for transfers between devices, tell_stages_all_on(): later = jax.lax.all_gather(local_x, 'orb')  28.9 us
    dot_general x1, matrix products, body(): jnp.einsum('bo,bc->oc', listed, basis_values, preferred_element_type=jnp....  17.4 us
    gather x1, local copies, waits for them, and re-layouts, body(): taken = jnp.take(shard_rows, safe_rows, axis=0)  8.65 us
    ppermute x1, waiting for transfers between devices, with_halo(): lax.ppermute(tail, axis, [(i, (i + 1) % count) for i in range(ends)])  3.48 us
  transfers between devices with their start and end apart: 4, of which 3 were waited for; matrix products, arithmetic and copies ran while one was open for 1% of the time, Pallas kernels for 0%

profile of v1, /device:TPU:4, one launch (start us, length us, event | category | flops | bytes accessed | tf_op | source)
XLA Modules:
  0.0 173.1 jit_solution(10452355087205392284)
XLA Ops:
  7.2 0.0 all-gather.3.cloned.1.call-start
  7.2 2.7 %copy.8 = bf16[8192,32]{1,0:T(8,128)(2,1)} copy(bf16[8192,32]{0,1:T(8,128)(2,1)} %param.6) | data formatting | bytes 1048576 | tf_op args[1]
  9.9 0.0 all-gather.3.cloned.1.call-update
  9.9 0.0 all-gather.5.cloned.1.call-start
  10.0 0.7 broadcast_multiply_fusion
  10.6 0.7 compare_and_fusion
  11.3 88.9 %all-gather.3.cloned.1.call-done = bf16[65536,32]{1,0:T(8,128)(2,1)} async-done(((bf16[8192,32]{1,0:T(8,128)(2,1)}), bf16[65536,32]{1,0:T(8,128)(2,1)}) %all-gather.3.cloned.1.call-update) | async-done | bytes 4194320 | tf_op jit(solution)/shard_map/all_gather | solution.py:47
  100.3 8.7 %gather_fusion = bf16[256,32]{1,0:T(8,128)(2,1)S(1)} fusion(bf16[65536,32]{1,0:T(8,128)(2,1)} %all-gather.3.cloned.1.call-done, s32[1024]{0:T(1024)S(1)} %pad_clamp_fusion), kind=kCustom, calls=%fused_computation | custom fusion | bytes 33792 | tf_op jit(solution)/shard_map/jit(_take)/gather | solution.py:50
  108.9 17.4 %fusion = f32[65536]{0:T(1024)} fusion(f32[32]{0:T(128)} %param.7, bf16[256,65536]{1,0:T(8,128)(2,1)} %param.5, bf16[256,32]{1,0:T(8,128)(2,1)S(1)} %gather_fusion, pred[256]{0:T(512)(128)(4,1)S(1)} %get-tuple-element.2, pred[256]{0:T(512)(128)(4,1)S(1)} %get-tuple-element.8), kind=kOutput, calls=%fused_computation.2 | convolution fusion | flops 1079984128 | bytes 33833600 | tf_op jit(solution)/shard_map/bo,bc->oc/dot_general | solution.py:54
  126.3 0.0 all-gather.5.cloned.1.call-update
  126.4 28.9 %all-gather.5.cloned.1.call-done = f32[4,8,64,128]{3,2,1,0:T(8,128)} async-done(((f32[1,8,64,128]{3,2,1,0:T(8,128)}), f32[4,8,64,128]{3,2,1,0:T(8,128)}) %all-gather.5.cloned.1.call-update) | async-done | bytes 1048592 | tf_op jit(solution)/shard_map/all_gather | solution.py:11
  155.2 1.3 reduce_sum.19
  156.5 2.3 %collective-permute-start = (f32[1,64,128]{2,1,0:T(8,128)S(1)}, f32[1,64,128]{2,1,0:T(8,128)S(1)}, u32[]{:S(2)}, u32[]{:S(2)}) collective-permute-start(f32[1,64,128]{2,1,0:T(8,128)S(1)} %get-tuple-element.6), channel_id=1, source_target_pairs={{1,0},{2,1},{3,2},{4,3},{5,4},{6,5},{7,6},{9,8},{10,9},{11,10},{12... | collective-permute-start | bytes 98312 | tf_op jit(solution)/shard_map/ppermute | solution.py:26
  158.9 2.0 %collective-permute-start.1 = (f32[1,64,128]{2,1,0:T(8,128)S(1)}, f32[1,64,128]{2,1,0:T(8,128)S(1)}, u32[]{:S(2)}, u32[]{:S(2)}) collective-permute-start(f32[1,64,128]{2,1,0:T(8,128)S(1)} %get-tuple-element.7), channel_id=1, source_target_pairs={{0,1},{1,2},{2,3},{3,4},{4,5},{5,6},{6,7},{8,9},{9,10},{10,11},{11... | collective-permute-start | bytes 98312 | tf_op jit(solution)/shard_map/ppermute | solution.py:24
  160.9 0.6 constant_dynamic-slice_fusion
  161.5 0.0 collective-permute-done
  161.5 3.5 %collective-permute-done.1 = f32[1,64,128]{2,1,0:T(8,128)S(1)} collective-permute-done((f32[1,64,128]{2,1,0:T(8,128)S(1)}, f32[1,64,128]{2,1,0:T(8,128)S(1)}, u32[]{:S(2)}, u32[]{:S(2)}) %collective-permute-start.1) | collective-permute-done | bytes 32800 | tf_op jit(solution)/shard_map/ppermute | solution.py:24
  165.0 0.3 select_maximum_fusion
  165.3 0.3 fusion.5
  165.6 0.7 fusion.12
  (2 shorter events, 0.0 us)
Async XLA Ops:
  7.2 93.1 %all-gather.3.cloned.1.call-start = ((), (), s32[]{:S(2)}) async-start(), calls=%async_computation | async-start | bytes 18874368 | tf_op jit(solution)/shard_map/all_gather | solution.py:47
  9.9 145.3 %all-gather.5.cloned.1.call-start = ((), (), s32[]{:S(2)}) async-start(), calls=%async_computation.1 | async-start | bytes 1310720 | tf_op jit(solution)/shard_map/all_gather | solution.py:11
  156.5 5.0 %collective-permute-start = (f32[1,64,128]{2,1,0:T(8,128)S(1)}, f32[1,64,128]{2,1,0:T(8,128)S(1)}, u32[]{:S(2)}, u32[]{:S(2)}) collective-permute-start(f32[1,64,128]{2,1,0:T(8,128)S(1)} %get-tuple-element.6), channel_id=1, source_target_pairs={{1,0},{2,1},{3,2},{4,3},{5,4},{6,5},{7,6},{9,8},{10,9},{11,10},{12... | collective-permute-start | bytes 98312 | tf_op jit(solution)/shard_map/ppermute | solution.py:26
  158.9 6.1 %collective-permute-start.1 = (f32[1,64,128]{2,1,0:T(8,128)S(1)}, f32[1,64,128]{2,1,0:T(8,128)S(1)}, u32[]{:S(2)}, u32[]{:S(2)}) collective-permute-start(f32[1,64,128]{2,1,0:T(8,128)S(1)} %get-tuple-element.7), channel_id=1, source_target_pairs={{0,1},{1,2},{2,3},{3,4},{4,5},{5,6},{6,7},{8,9},{9,10},{10,11},{11... | collective-permute-start | bytes 98312 | tf_op jit(solution)/shard_map/ppermute | solution.py:24
Sparse Core Ops, SparseCore 0:
  10.0 90.1 all-gather.2
  126.5 28.7 all-gather.4
